TPU v7x, 32 devices: a whole 2x2x4 slice. The times are simulated.
32 devices in a mesh: dp: 16 (over z, y, x), mp: 2 (over core).
Axes of the slice: x: 2, y: 2, z: 4, core: 2. Of those that a mesh axis runs over, the one named last changes fastest.
Arguments:
- hidden: bfloat16 [2, 64, 64, 768], P(None, 'dp'), may hold values from -6 to 6
- encoder_tokens: bfloat16 [2, 32, 576, 768], P(None, 'dp'), may hold values from -6 to 6
- segment_ids: int32 [2, 64, 64], P(None, 'dp'), may hold values from 0 to 3, never falling along the last dimension, each value on 1 to 32 neighbouring positions
- image_index: int32 [2, 64], P(None, 'dp'), may hold values from 0 to 1
- cotangent: bfloat16 [2, 64, 64, 768], P(None, 'dp'), may hold values from -6 to 6
- norm_gains: bfloat16 [3, 768], P(None, 'dp'), may hold values from 0.099609375 to 1.8984375
- qkv_weight: bfloat16 [3, 768, 768], P(None, 'dp', 'mp'), may hold values from -0.21875 to 0.21875
- self_out_weight: bfloat16 [768, 768], P('dp', 'mp'), may hold values from -0.875 to 0.875
- cross_query_weight: bfloat16 [768, 768], P('dp', 'mp'), may hold values from -0.21875 to 0.21875
- cross_kv_weight: bfloat16 [2, 768, 768], P(None, 'dp', 'mp'), may hold values from -0.21875 to 0.21875
- cross_out_weight: bfloat16 [768, 768], P('dp', 'mp'), may hold values from -2.5 to 2.5
- up_weight: bfloat16 [768, 3072], P('dp', 'mp'), may hold values from -0.21875 to 0.21875
- down_weight: bfloat16 [768, 3072], P('dp', 'mp'), may hold values from -0.109375 to 0.109375
Outputs:
- output: bfloat16 [2, 64, 64, 768], P(None, 'dp')
- input_grad: float32 [2, 64, 64, 768], P(None, 'dp')
- encoder_grad: float32 [2, 32, 576, 768], P(None, 'dp', None, 'mp')
- grad_norm_gains: float32 [3, 768], P(None, 'dp')
- grad_qkv: float32 [3, 768, 768], P(None, 'dp', 'mp')
- grad_self_out: float32 [768, 768], P('dp', 'mp')
- grad_cross_query: float32 [768, 768], P('dp', 'mp')
- grad_cross_kv: float32 [2, 768, 768], P(None, 'dp', 'mp')
- grad_cross_out: float32 [768, 768], P('dp', 'mp')
- grad_up: float32 [768, 3072], P('dp', 'mp')
- grad_down: float32 [768, 3072], P('dp', 'mp')
Inputs may be any that keep to these rules, and one draw needn't show every extreme that they name: `segment_ids`: within a row the ids never fall; they number the 4 captions of the row, each of 1 to 32 tokens. Caption row r of a micro-batch reads image (r // 4) * 2 + image_index of that row.
All inputs are finite; a program needn't handle non-finite values.
Results may differ from a plain program's by a relative error of at most 0.019.
Values may be sent and summed in bfloat16 or wider, within the bound.
A program may use at most 192 MiB of HBM per device.

v0:
```python
import jax
import jax.numpy as jnp
from jax import lax
from jax.sharding import PartitionSpec as P

HEAD = 64
EPSILON = 1e-05
NEGATIVE = -1e30


def layer_norm(values, gain_row):
    centred = values - jnp.mean(values, axis=-1, keepdims=True)
    spread = jnp.mean(centred * centred, axis=-1, keepdims=True)
    return centred * lax.rsqrt(spread + EPSILON) * gain_row


def gelu_exact(values):
    return jax.nn.gelu(values, approximate=False)


def token_outer(left, right):
    return lax.dot_general(
        left, right, (((0,), (0,)), ((), ())), preferred_element_type=jnp.float32
    )


def feature_inner(left, right):
    return lax.dot_general(
        left, right, (((1,), (1,)), ((), ())), preferred_element_type=jnp.float32
    )


def attend(queries, key_heads, value_heads, allowed, score_scale):
    scores = (
        jnp.einsum("rqhe,rkhe->rhqk", queries, key_heads, preferred_element_type=jnp.float32)
        * score_scale
    )
    if allowed is not None:
        scores = jnp.where(allowed[:, None], scores, NEGATIVE)
    row_max = jnp.max(scores, axis=-1, keepdims=True)
    shifted = jnp.exp(scores - row_max)
    row_total = jnp.sum(shifted, axis=-1, keepdims=True)
    weights_low = (shifted / row_total).astype(jnp.bfloat16)
    mixed_heads = jnp.einsum(
        "rhqk,rkhe->rqhe", weights_low, value_heads, preferred_element_type=jnp.float32
    )
    return (mixed_heads.astype(jnp.bfloat16), row_max + jnp.log(row_total))


def attend_back(queries, key_heads, value_heads, allowed, score_scale, log_total, grad_mixed):
    scores = (
        jnp.einsum("rqhe,rkhe->rhqk", queries, key_heads, preferred_element_type=jnp.float32)
        * score_scale
    )
    if allowed is not None:
        scores = jnp.where(allowed[:, None], scores, NEGATIVE)
    probability = jnp.exp(scores - log_total)
    grad_weights = jnp.einsum(
        "rqhe,rkhe->rhqk", grad_mixed, value_heads, preferred_element_type=jnp.float32
    )
    inner_sum = jnp.sum(probability * grad_weights, axis=-1, keepdims=True)
    grad_scores = (probability * (grad_weights - inner_sum)).astype(jnp.bfloat16)
    grad_queries = (
        jnp.einsum("rhqk,rkhe->rqhe", grad_scores, key_heads, preferred_element_type=jnp.float32)
        * score_scale
    )
    grad_keys = (
        jnp.einsum("rhqk,rqhe->rkhe", grad_scores, queries, preferred_element_type=jnp.float32)
        * score_scale
    )
    grad_values = jnp.einsum(
        "rhqk,rqhe->rkhe",
        probability.astype(jnp.bfloat16),
        grad_mixed,
        preferred_element_type=jnp.float32,
    )
    return (grad_queries, grad_keys, grad_values)


def fetch_weights(
    norm_gains,
    qkv_weight,
    self_out_weight,
    cross_query_weight,
    cross_kv_weight,
    cross_out_weight,
    up_weight,
    down_weight,
):
    return (
        lax.all_gather(norm_gains, "dp", axis=1, tiled=True),
        lax.all_gather(qkv_weight, "dp", axis=1, tiled=True),
        lax.all_gather(self_out_weight, "dp", axis=0, tiled=True),
        lax.all_gather(cross_query_weight, "dp", axis=0, tiled=True),
        lax.all_gather(cross_kv_weight, "dp", axis=1, tiled=True),
        lax.all_gather(cross_out_weight, "dp", axis=0, tiled=True),
        lax.all_gather(up_weight, "dp", axis=0, tiled=True),
        lax.all_gather(down_weight, "dp", axis=0, tiled=True),
    )


def reduce_weight_grads(gradients):
    return (
        lax.psum_scatter(gradients[0], "dp", scatter_dimension=1, tiled=True),
        lax.psum_scatter(gradients[1], "dp", scatter_dimension=1, tiled=True),
        lax.psum_scatter(gradients[2], "dp", scatter_dimension=0, tiled=True),
        lax.psum_scatter(gradients[3], "dp", scatter_dimension=0, tiled=True),
        lax.psum_scatter(gradients[4], "dp", scatter_dimension=1, tiled=True),
        lax.psum_scatter(gradients[5], "dp", scatter_dimension=0, tiled=True),
        lax.psum_scatter(gradients[6], "dp", scatter_dimension=0, tiled=True),
        lax.psum_scatter(gradients[7], "dp", scatter_dimension=0, tiled=True),
    )


def branch_output(mixed_heads, weight):
    return lax.psum(feature_inner(mixed_heads, weight), "mp")


def input_grad_sum(partial_sum):
    return lax.psum(partial_sum.astype(jnp.bfloat16), "mp").astype(jnp.float32)


def add_pair(first, second):
    return first + second


def micro_step(gathered, hidden, encoder, segment, image_ids, cotangent):
    (
        norm_gains,
        qkv_weight,
        self_out_weight,
        cross_query_weight,
        cross_kv_weight,
        cross_out_weight,
        up_weight,
        down_weight,
    ) = gathered
    row_count, length, model_width = hidden.shape
    image_count, context = (encoder.shape[0], encoder.shape[1])
    head_count = qkv_weight.shape[2] // HEAD
    tokens = row_count * length
    head_shape = (row_count, length, head_count, HEAD)
    score_scale = HEAD ** (-0.5)
    gain_rows = norm_gains.astype(jnp.float32)
    positions = jnp.arange(length)
    causal = positions[None, :] <= positions[:, None]
    allowed = causal[None] & (segment[:, :, None] == segment[:, None, :])
    flat_in = hidden.reshape(tokens, model_width).astype(jnp.float32)
    low_one = layer_norm(flat_in, gain_rows[0]).astype(jnp.bfloat16)
    projected = jnp.einsum(
        "td,jde->jte", low_one, qkv_weight, preferred_element_type=jnp.float32
    ).astype(jnp.bfloat16)
    queries = projected[0].reshape(head_shape)
    key_heads = projected[1].reshape(head_shape)
    value_heads = projected[2].reshape(head_shape)
    self_mixed, self_total = attend(queries, key_heads, value_heads, allowed, score_scale)
    self_flat = self_mixed.reshape(tokens, -1)
    resid_one = flat_in + branch_output(self_flat, self_out_weight)
    low_two = layer_norm(resid_one, gain_rows[1]).astype(jnp.bfloat16)
    cross_queries = (
        jnp.dot(low_two, cross_query_weight, preferred_element_type=jnp.float32)
        .astype(jnp.bfloat16)
        .reshape(head_shape)
    )
    image_kv = jnp.einsum(
        "ncd,jde->jnce", encoder, cross_kv_weight, preferred_element_type=jnp.float32
    ).astype(jnp.bfloat16)
    row_kv = jnp.take(image_kv, image_ids, axis=1).reshape(2, row_count, context, head_count, HEAD)
    cross_mixed, cross_total = attend(cross_queries, row_kv[0], row_kv[1], None, score_scale)
    cross_flat = cross_mixed.reshape(tokens, -1)
    resid_two = resid_one + branch_output(cross_flat, cross_out_weight)
    low_three = layer_norm(resid_two, gain_rows[2]).astype(jnp.bfloat16)
    pre_act = jnp.dot(low_three, up_weight, preferred_element_type=jnp.float32)
    activated = gelu_exact(pre_act).astype(jnp.bfloat16)
    resid_three = resid_two + branch_output(activated, down_weight)
    output_rows = resid_three.astype(jnp.bfloat16).reshape(row_count, length, model_width)
    grad_low = cotangent.reshape(tokens, model_width)
    grad_down = token_outer(grad_low, activated)
    grad_act = jnp.dot(grad_low, down_weight, preferred_element_type=jnp.float32)
    gelu_back = jax.vjp(gelu_exact, pre_act)[1]
    grad_pre = gelu_back(grad_act)[0].astype(jnp.bfloat16)
    grad_up = token_outer(low_three, grad_pre)
    grad_normed = input_grad_sum(feature_inner(grad_pre, up_weight))
    norm_back = jax.vjp(layer_norm, resid_two, gain_rows[2])[1]
    grad_resid, grad_gain_three = norm_back(grad_normed)
    grad_two = grad_low.astype(jnp.float32) + grad_resid
    low_grad_two = grad_two.astype(jnp.bfloat16)
    grad_cross_out = token_outer(low_grad_two, cross_flat)
    grad_cross_mixed = (
        jnp.dot(low_grad_two, cross_out_weight, preferred_element_type=jnp.float32)
        .astype(jnp.bfloat16)
        .reshape(head_shape)
    )
    grad_cq, grad_ck, grad_cv = attend_back(
        cross_queries, row_kv[0], row_kv[1], None, score_scale, cross_total, grad_cross_mixed
    )
    low_cq = grad_cq.reshape(tokens, -1).astype(jnp.bfloat16)
    chooser = (image_ids[:, None] == jnp.arange(image_count)[None, :]).astype(jnp.float32)
    grad_rows_kv = jnp.stack([grad_ck, grad_cv]).reshape(2, row_count, context, -1)
    grad_image_kv = jnp.einsum(
        "ri,jrce->jice", chooser, grad_rows_kv, precision=lax.Precision.HIGHEST
    ).astype(jnp.bfloat16)
    grad_cross_query = token_outer(low_two, low_cq)
    grad_cross_kv = jnp.einsum(
        "ncd,jnce->jde", encoder, grad_image_kv, preferred_element_type=jnp.float32
    )
    encoder_part = jnp.einsum(
        "jnce,jde->ncd", grad_image_kv, cross_kv_weight, preferred_element_type=jnp.float32
    )
    encoder_grad = lax.psum_scatter(
        encoder_part.astype(jnp.bfloat16), "mp", scatter_dimension=2, tiled=True
    ).astype(jnp.float32)
    grad_normed = input_grad_sum(feature_inner(low_cq, cross_query_weight))
    norm_back = jax.vjp(layer_norm, resid_one, gain_rows[1])[1]
    grad_resid, grad_gain_two = norm_back(grad_normed)
    grad_one = grad_two + grad_resid
    low_grad_one = grad_one.astype(jnp.bfloat16)
    grad_self_out = token_outer(low_grad_one, self_flat)
    grad_self_mixed = (
        jnp.dot(low_grad_one, self_out_weight, preferred_element_type=jnp.float32)
        .astype(jnp.bfloat16)
        .reshape(head_shape)
    )
    grad_sq, grad_sk, grad_sv = attend_back(
        queries, key_heads, value_heads, allowed, score_scale, self_total, grad_self_mixed
    )
    grad_projected = (
        jnp.stack([grad_sq, grad_sk, grad_sv]).reshape(3, tokens, -1).astype(jnp.bfloat16)
    )
    grad_qkv = jnp.einsum(
        "td,jte->jde", low_one, grad_projected, preferred_element_type=jnp.float32
    )
    grad_normed = input_grad_sum(
        jnp.einsum("jte,jde->td", grad_projected, qkv_weight, preferred_element_type=jnp.float32)
    )
    norm_back = jax.vjp(layer_norm, flat_in, gain_rows[0])[1]
    grad_resid, grad_gain_one = norm_back(grad_normed)
    input_rows = (grad_one + grad_resid).reshape(row_count, length, model_width)
    grad_gains = jnp.stack([grad_gain_one, grad_gain_two, grad_gain_three])
    gradients = (
        grad_gains,
        grad_qkv,
        grad_self_out,
        grad_cross_query,
        grad_cross_kv,
        grad_cross_out,
        grad_up,
        grad_down,
    )
    return (output_rows, input_rows, encoder_grad, gradients)


def body(
    hidden,
    encoder_tokens,
    segment_ids,
    image_index,
    cotangent,
    norm_gains,
    qkv_weight,
    self_out_weight,
    cross_query_weight,
    cross_kv_weight,
    cross_out_weight,
    up_weight,
    down_weight,
):
    micro_count = hidden.shape[0]
    gathered = None
    outputs = []
    input_grads = []
    encoder_grads = []
    reduced = None
    for micro_index in range(micro_count):
        gathered = fetch_weights(
            norm_gains,
            qkv_weight,
            self_out_weight,
            cross_query_weight,
            cross_kv_weight,
            cross_out_weight,
            up_weight,
            down_weight,
        )
        output_rows, input_rows, encoder_rows, gradients = micro_step(
            gathered,
            hidden[micro_index],
            encoder_tokens[micro_index],
            segment_ids[micro_index],
            image_index[micro_index],
            cotangent[micro_index],
        )
        outputs.append(output_rows)
        input_grads.append(input_rows)
        encoder_grads.append(encoder_rows)
        shards = reduce_weight_grads(gradients)
        reduced = shards if reduced is None else jax.tree.map(add_pair, reduced, shards)
    return (
        jnp.stack(outputs),
        jnp.stack(input_grads),
        jnp.stack(encoder_grads),
        reduced[0],
        reduced[1],
        reduced[2],
        reduced[3],
        reduced[4],
        reduced[5],
        reduced[6],
        reduced[7],
    )


def solution(mesh):
    placed = (
        P(None, "dp", None, None),
        P(None, "dp", None, None),
        P(None, "dp", None),
        P(None, "dp"),
        P(None, "dp", None, None),
        P(None, "dp"),
        P(None, "dp", "mp"),
        P("dp", "mp"),
        P("dp", "mp"),
        P(None, "dp", "mp"),
        P("dp", "mp"),
        P("dp", "mp"),
        P("dp", "mp"),
    )
    return jax.shard_map(
        body,
        mesh=mesh,
        in_specs=placed,
        out_specs=(
            P(None, "dp", None, None),
            P(None, "dp", None, None),
            P(None, "dp", None, "mp"),
            P(None, "dp"),
            P(None, "dp", "mp"),
            P("dp", "mp"),
            P("dp", "mp"),
            P(None, "dp", "mp"),
            P("dp", "mp"),
            P("dp", "mp"),
            P("dp", "mp"),
        ),
        check_vma=False,
    )
```

profile of v0, /device:TPU:0, one launch (start us, length us, event | category | flops | bytes accessed | tf_op | source)
XLA Modules:
  0.0 1708.3 jit_solution(6245522283395078489)
XLA Ops:
  11.9 42.4 %all-gather = bf16[16,48,3]{1,2,0:T(4,128)(2,1)S(1)} all-gather(bf16[1,48,3]{1,2,0:T(4,128)(2,1)S(1)} %bitcast.350), channel_id=1, replica_groups=mesh['dp'=16,'mp'=2] {'dp'}, dimensions={0}, use_global_device_ids=true | all-gather | bytes 4896 | tf_op jit(solution)/shard_map/all_gather | solution.py:91
  56.9 40.3 %all_gather.34 = bf16[768,384]{1,0:T(8,128)(2,1)S(1)} all-gather(bf16[48,384]{1,0:T(8,128)(2,1)S(1)} %copy-done.100), channel_id=1, replica_groups=mesh['dp'=16,'mp'=2] {'dp'}, dimensions={0}, use_global_device_ids=true | all-gather | bytes 626688 | tf_op jit(solution)/shard_map/all_gather | solution.py:93
  97.3 44.4 %all_gather.36 = bf16[768,384]{1,0:T(8,128)(2,1)} all-gather(bf16[48,384]{1,0:T(8,128)(2,1)S(1)} %copy-done.101), channel_id=1, replica_groups=mesh['dp'=16,'mp'=2] {'dp'}, dimensions={0}, use_global_device_ids=true | all-gather | bytes 626688 | tf_op jit(solution)/shard_map/all_gather | solution.py:94
  141.7 40.7 %all_gather.37 = bf16[768,384]{1,0:T(8,128)(2,1)S(1)} all-gather(bf16[48,384]{1,0:T(8,128)(2,1)S(1)} %copy-done.102), channel_id=1, replica_groups=mesh['dp'=16,'mp'=2] {'dp'}, dimensions={0}, use_global_device_ids=true | all-gather | bytes 626688 | tf_op jit(solution)/shard_map/all_gather | solution.py:96
  281.2 14.4 all-reduce.21.cloned.1.call-done
  300.1 61.7 %all-gather.10.cloned.1.call-done = bf16[768,1536]{1,0:T(8,128)(2,1)} async-done(((bf16[48,1536]{1,0:T(8,128)(2,1)}), bf16[768,1536]{1,0:T(8,128)(2,1)}) %all-gather.10.cloned.1.call-update) | async-done | bytes 2359312 | tf_op jit(solution)/shard_map/all_gather | solution.py:97
  365.7 59.9 %all-gather.12.cloned.1.call-done = bf16[768,1536]{1,0:T(8,128)(2,1)} async-done(((bf16[48,1536]{1,0:T(8,128)(2,1)}), bf16[768,1536]{1,0:T(8,128)(2,1)}) %all-gather.12.cloned.1.call-update) | async-done | bytes 2359312 | tf_op jit(solution)/shard_map/all_gather | solution.py:98
  425.6 6.4 add_convert_fusion
  437.4 5.1 add_convert_fusion.1
  456.9 6.3 all-reduce.29.cloned.1.call-done
  468.4 19.6 %all-reduce.19.cloned.1.call-done = (f32[256,768]{1,0:T(8,128)}, f32[256,768]{1,0:T(8,128)}) async-done(((f32[256,768]{1,0:T(8,128)}, f32[256,768]{1,0:T(8,128)}), (f32[256,768]{1,0:T(8,128)}, f32[256,768]{1,0:T(8,128)})) %all-reduce.19.cloned.1.call-update) | async-done | bytes 1572880 | tf_op jit(solution)/shard_map/psum | solution.py:116
  541.5 5.1 fusion.27
  546.6 6.3 copy.329
  622.6 6.2 copy.328
  628.8 10.9 fusion.16
  653.9 6.6 copy.374
  670.6 6.1 copy.334
  681.0 6.2 copy.333
  687.1 10.1 fusion.19
  701.3 6.6 copy.376
  707.8 5.0 reshape.451
  720.3 5.3 copy.341
  730.1 6.2 copy.338
  757.0 6.1 copy.380
  773.5 9.2 reduce-scatter.25.cloned.1.call-done
  787.2 8.2 reduce-scatter.27.cloned.1.call-done
  801.9 229.5 %all-reduce.17.cloned.1.call-done = (f32[3,768,384]{2,0,1:T(4,128)}, f32[2,768,384]{2,0,1:T(2,128)}) async-done(((f32[3,768,384]{2,0,1:T(4,128)}, f32[2,768,384]{2,0,1:T(2,128)}), (f32[3,768,384]{2,0,1:T(4,128)}, f32[2,768,384]{2,0,1:T(2,128)})) %all-reduce.17.cloned.1.call-update) | async-done | bytes 5898256
  1034.8 125.2 %reduce-scatter.21.cloned.1.call-done = f32[48,384]{1,0:T(8,128)} async-done(((f32[768,384]{1,0:T(8,128)}), f32[48,384]{1,0:T(8,128)}) %reduce-scatter.21.cloned.1.call-update) | async-done | bytes 73744 | tf_op jit(solution)/shard_map/reduce_scatter | solution.py:109
  1159.9 128.6 %reduce-scatter.19.cloned.1.call-done = f32[48,384]{1,0:T(8,128)} async-done(((f32[768,384]{1,0:T(8,128)}), f32[48,384]{1,0:T(8,128)}) %reduce-scatter.19.cloned.1.call-update) | async-done | bytes 73744 | tf_op jit(solution)/shard_map/reduce_scatter | solution.py:107
  1288.5 128.5 %reduce-scatter.17.cloned.1.call-done = f32[48,384]{1,0:T(8,128)} async-done(((f32[768,384]{1,0:T(8,128)}), f32[48,384]{1,0:T(8,128)}) %reduce-scatter.17.cloned.1.call-update) | async-done | bytes 73744 | tf_op jit(solution)/shard_map/reduce_scatter | solution.py:106
  1417.0 142.4 %reduce-scatter.23.cloned.1.call-done = f32[48,1536]{1,0:T(8,128)} async-done(((f32[768,1536]{1,0:T(8,128)}), f32[48,1536]{1,0:T(8,128)}) %reduce-scatter.23.cloned.1.call-update) | async-done | bytes 294928 | tf_op jit(solution)/shard_map/reduce_scatter | solution.py:110
  1559.5 141.9 %reduce-scatter.31.cloned.1.call-done = f32[48,1536]{1,0:T(8,128)} async-done(((f32[768,1536]{1,0:T(8,128)}), f32[48,1536]{1,0:T(8,128)}) %reduce-scatter.31.cloned.1.call-update) | async-done | bytes 294928
  (554 shorter events, 350.0 us)
Async XLA Ops:
  7.2 48.7 %copy-start.4 = (bf16[2,4,64,768]{3,2,1,0:T(8,128)(2,1)S(1)}, bf16[2,4,64,768]{3,2,1,0:T(8,128)(2,1)}, u32[]{:S(2)}) copy-start(bf16[2,4,64,768]{3,2,1,0:T(8,128)(2,1)} %param.15) | copy-start | bytes 2359300
  7.2 47.3 %copy-start.130 = (s32[2,4]{1,0:T(2,128)S(1)}, s32[2,4]{1,0:T(2,128)}, u32[]{:S(2)}) copy-start(s32[2,4]{1,0:T(2,128)} %param.18) | copy-start | bytes 100
  7.2 47.9 %copy-start.131 = (s32[2,4,64]{2,1,0:T(4,128)S(1)}, s32[2,4,64]{2,1,0:T(4,128)}, u32[]{:S(2)}) copy-start(s32[2,4,64]{2,1,0:T(4,128)} %param.17) | copy-start | bytes 6148
  7.2 175.2 %all-gather.8.cloned.1.call-start = ((), (), s32[]{:S(2)}) async-start(), calls=%async_computation.9 | async-start | bytes 1253376 | tf_op jit(solution)/shard_map/all_gather | solution.py:95
  8.0 49.0 %copy-start.100 = (bf16[48,384]{1,0:T(8,128)(2,1)S(1)}, bf16[48,384]{1,0:T(8,128)(2,1)}, u32[]{:S(2)}) copy-start(bf16[48,384]{1,0:T(8,128)(2,1)} %param.22) | copy-start | bytes 110596
  8.0 183.6 %all-gather.6.cloned.1.call-start = ((), (), s32[]{:S(2)}) async-start(), calls=%async_computation.8 | async-start | bytes 1880064 | tf_op jit(solution)/shard_map/all_gather | solution.py:92
  8.7 239.7 %all-reduce.23.cloned.1.call-start = ((), (), s32[]{:S(2)}) async-start(), calls=%async_computation.23 | async-start | bytes 3145728 | tf_op jit(solution)/shard_map/psum | solution.py:116
  10.1 87.2 %copy-start.101 = (bf16[48,384]{1,0:T(8,128)(2,1)S(1)}, bf16[48,384]{1,0:T(8,128)(2,1)}, u32[]{:S(2)}) copy-start(bf16[48,384]{1,0:T(8,128)(2,1)} %param.23) | copy-start | bytes 110596
  10.1 131.6 %copy-start.102 = (bf16[48,384]{1,0:T(8,128)(2,1)S(1)}, bf16[48,384]{1,0:T(8,128)(2,1)}, u32[]{:S(2)}) copy-start(bf16[48,384]{1,0:T(8,128)(2,1)} %param.25) | copy-start | bytes 110596
  11.7 170.7 %copy-start.107 = (f32[256]{0:T(256)}, f32[256]{0:T(256)S(1)}, u32[]{:S(2)}) copy-start(f32[256]{0:T(256)S(1)} %div.157) | copy-start | bytes 3076
  11.7 170.6 %copy-start.109 = (f32[256]{0:T(256)}, f32[256]{0:T(256)S(1)}, u32[]{:S(2)}) copy-start(f32[256]{0:T(256)S(1)} %div.168) | copy-start | bytes 3076
  11.8 170.5 %copy-start.113 = (f32[256]{0:T(256)}, f32[256]{0:T(256)S(1)}, u32[]{:S(2)}) copy-start(f32[256]{0:T(256)S(1)} %rsqrt.66) | copy-start | bytes 3076
  11.9 170.4 %copy-start.115 = (f32[256]{0:T(256)}, f32[256]{0:T(256)S(1)}, u32[]{:S(2)}) copy-start(f32[256]{0:T(256)S(1)} %rsqrt.69) | copy-start | bytes 3076
  56.9 134.6 %copy-start.67 = (bf16[256,768]{1,0:T(8,128)(2,1)}, bf16[256,768]{1,0:T(8,128)(2,1)S(1)}, u32[]{:S(2)}) copy-start(bf16[256,768]{1,0:T(8,128)(2,1)S(1)} %get-tuple-element.120) | copy-start | bytes 1179652
  97.3 115.6 %copy-start.15 = (bf16[768,384]{1,0:T(8,128)(2,1)}, bf16[768,384]{1,0:T(8,128)(2,1)S(1)}, u32[]{:S(2)}) copy-start(bf16[768,384]{1,0:T(8,128)(2,1)S(1)} %all_gather.34) | copy-start | bytes 1769476
  182.4 95.4 %copy-start.18 = (bf16[768,384]{1,0:T(8,128)(2,1)}, bf16[768,384]{1,0:T(8,128)(2,1)S(1)}, u32[]{:S(2)}) copy-start(bf16[768,384]{1,0:T(8,128)(2,1)S(1)} %all_gather.37) | copy-start | bytes 1769476
  214.2 81.4 %all-reduce.21.cloned.1.call-start = ((), (), s32[]{:S(2)}) async-start(), calls=%async_computation.22 | async-start | bytes 3145728 | tf_op jit(solution)/shard_map/psum | solution.py:116
  279.1 82.6 %all-gather.10.cloned.1.call-start = ((), (), s32[]{:S(2)}) async-start(), calls=%async_computation.10 | async-start | bytes 2506752 | tf_op jit(solution)/shard_map/all_gather | solution.py:97
  279.7 145.8 %all-gather.12.cloned.1.call-start = ((), (), s32[]{:S(2)}) async-start(), calls=%async_computation.11 | async-start | bytes 2506752 | tf_op jit(solution)/shard_map/all_gather | solution.py:98
  280.3 183.0 %all-reduce.29.cloned.1.call-start = ((), (), s32[]{:S(2)}) async-start(), calls=%async_computation.26 | async-start | bytes 1572864 | tf_op jit(solution)/shard_map/psum | solution.py:120
  445.0 43.0 %all-reduce.19.cloned.1.call-start = ((), (), s32[]{:S(2)}) async-start(), calls=%async_computation.21 | async-start | bytes 3145728 | tf_op jit(solution)/shard_map/psum | solution.py:116
  452.7 104.1 %all-reduce.27.cloned.1.call-start = ((), (), s32[]{:S(2)}) async-start(), calls=%async_computation.25 | async-start | bytes 1572864 | tf_op jit(solution)/shard_map/psum | solution.py:120
  536.2 104.7 %all-reduce.25.cloned.1.call-start = ((), (), s32[]{:S(2)}) async-start(), calls=%async_computation.24 | async-start | bytes 1572864 | tf_op jit(solution)/shard_map/psum | solution.py:120
  617.9 154.1 %reduce-scatter.29.cloned.1.call-start = ((), (), s32[]{:S(2)}) async-start(), calls=%async_computation.18 | async-start | bytes 417792
  649.1 133.5 %reduce-scatter.25.cloned.1.call-start = ((), (), s32[]{:S(2)}) async-start(), calls=%async_computation.16 | async-start | bytes 2654208
  665.4 130.0 %reduce-scatter.27.cloned.1.call-start = ((), (), s32[]{:S(2)}) async-start(), calls=%async_computation.17 | async-start | bytes 2654208
  712.8 318.6 %all-reduce.17.cloned.1.call-start = ((), (), s32[]{:S(2)}) async-start(), calls=%async_computation.20 | async-start | bytes 14155776
  736.4 423.6 %reduce-scatter.21.cloned.1.call-start = ((), (), s32[]{:S(2)}) async-start(), calls=%async_computation.14 | async-start | bytes 1253376 | tf_op jit(solution)/shard_map/reduce_scatter | solution.py:109
  739.4 549.1 %reduce-scatter.19.cloned.1.call-start = ((), (), s32[]{:S(2)}) async-start(), calls=%async_computation.13 | async-start | bytes 1253376 | tf_op jit(solution)/shard_map/reduce_scatter | solution.py:107
  743.4 673.6 %reduce-scatter.17.cloned.1.call-start = ((), (), s32[]{:S(2)}) async-start(), calls=%async_computation.12 | async-start | bytes 1253376 | tf_op jit(solution)/shard_map/reduce_scatter | solution.py:106
  746.4 813.1 %reduce-scatter.23.cloned.1.call-start = ((), (), s32[]{:S(2)}) async-start(), calls=%async_computation.15 | async-start | bytes 5013504 | tf_op jit(solution)/shard_map/reduce_scatter | solution.py:110
  751.8 949.5 %reduce-scatter.31.cloned.1.call-start = ((), (), s32[]{:S(2)}) async-start(), calls=%async_computation.19 | async-start | bytes 5013504
  (130 other events, 476.4 us)
Sparse Core Ops, SparseCore 0:
  10.7 59.4 all-gather.7
  72.9 61.2 all-gather.5
  214.3 16.3 all-reduce.22
  279.2 16.3 all-reduce.20
  298.3 63.4 all-gather.9
  364.4 61.0 all-gather.11
  445.1 18.0 all-reduce.28
  466.3 21.6 all-reduce.18
  536.3 20.4 all-reduce.26
  618.0 20.4 all-reduce.24
  649.3 122.7 reduce-scatter.28
  774.3 8.3 reduce-scatter.24
  784.9 10.4 reduce-scatter.26
  802.8 228.5 all-reduce.16
  1037.3 122.5 reduce-scatter.20
  1165.8 122.6 reduce-scatter.18
  1294.4 122.5 reduce-scatter.16
  1423.4 135.9 reduce-scatter.22
  1565.2 136.0 reduce-scatter.30
where the time goes:
time: 1720 us; the launch traced here: 1710 us
  waiting for transfers between devices  1080 us (63%)
  local copies, waits for them, and re-layouts  209 us (12%)
  matrix products  169 us (10%)
  blocking collectives  168 us (10%)
  other arithmetic  59.6 us (3%)
    unnamed x24, waiting for transfers between devices  392 us
    reduce_scatter x1, waiting for transfers between devices, reduce_weight_grads(): lax.psum_scatter(gradients[6], 'dp', scatter_dimension=0, tiled=True)  142 us
    reduce_scatter x1, waiting for transfers between devices, reduce_weight_grads(): lax.psum_scatter(gradients[3], 'dp', scatter_dimension=0, tiled=True)  129 us
    reduce_scatter x1, waiting for transfers between devices, reduce_weight_grads(): lax.psum_scatter(gradients[2], 'dp', scatter_dimension=0, tiled=True)  128 us
    reduce_scatter x1, waiting for transfers between devices, reduce_weight_grads(): lax.psum_scatter(gradients[5], 'dp', scatter_dimension=0, tiled=True)  125 us
    unnamed x306, local copies, waits for them, and re-layouts  68.8 us
    all_gather x1, waiting for transfers between devices, fetch_weights(): lax.all_gather(up_weight, 'dp', axis=0, tiled=True)  61.7 us
    all_gather x1, waiting for transfers between devices, fetch_weights(): lax.all_gather(down_weight, 'dp', axis=0, tiled=True)  59.9 us
  transfers between devices with their start and end apart: 19, of which 15 were waited for; matrix products, arithmetic and copies ran while one was open for 14% of the time, Pallas kernels for 0%

commit v1 on v0

--- a/solution.py
+++ b/solution.py
@@ -6,6 +6,25 @@
 HEAD = 64
 EPSILON = 1e-05
 NEGATIVE = -1e30
+
+
+def collect(x, axis, dim):
+    size, mine, span = (lax.axis_size(axis), lax.axis_index(axis), x.shape[dim])
+    upward = [(i, (i + 1) % size) for i in range(size)]
+    left = [(i, (i - 1) % size) for i in range(size)]
+    out = jnp.zeros((*x.shape[:dim], size * span, *x.shape[dim + 1 :]), x.dtype)
+    out = lax.dynamic_update_slice_in_dim(out, x, mine * span, axis=dim)
+    from_left = from_right = x
+    half = size // 2
+    for step in range(1, half + 1):
+        from_left = lax.ppermute(from_left, axis, upward)
+        out = lax.dynamic_update_slice_in_dim(out, from_left, (mine - step) % size * span, axis=dim)
+        if step < size - half:
+            from_right = lax.ppermute(from_right, axis, left)
+            out = lax.dynamic_update_slice_in_dim(
+                out, from_right, (mine + step) % size * span, axis=dim
+            )
+    return out
 
 
 def layer_norm(values, gain_row):
@@ -94,7 +113,7 @@
         lax.all_gather(cross_query_weight, "dp", axis=0, tiled=True),
         lax.all_gather(cross_kv_weight, "dp", axis=1, tiled=True),
         lax.all_gather(cross_out_weight, "dp", axis=0, tiled=True),
-        lax.all_gather(up_weight, "dp", axis=0, tiled=True),
+        collect(up_weight, "dp", 0),
         lax.all_gather(down_weight, "dp", axis=0, tiled=True),
     )
 

time: 1720 us -> 1670 us (0.971)
  waiting for transfers between devices: 1080 us -> 973 us
  starting transfers between devices: 2.2 us -> 39.5 us
    all_gather x1 -> x0, waiting for transfers between devices: 61.7 us -> none  [fetch_weights(): lax.all_gather(up_weight, 'dp', axis=0, tiled=True)]
    all_gather x1, waiting for transfers between devices: 59.9 us -> 0.01 us  [fetch_weights(): lax.all_gather(down_weight, 'dp', axis=0, tiled=True)]
    ppermute x0 -> x15, starting transfers between devices: none -> 37.5 us  [the longest x7 36.9 us: collect(): from_right = lax.ppermute(from_right, axis, left)]
    ppermute x0 -> x15, waiting for transfers between devices: none -> 30.3 us  [the longest x8 23 us: collect(): from_left = lax.ppermute(from_left, axis, upward)]
    unnamed x306 -> x302, local copies, waits for them, and re-layouts: 68.8 us -> 66.5 us
    unnamed x24 -> x23, waiting for transfers between devices: 392 us -> 391 us
  transfers between devices with their start and end apart: 19 -> 33, of which waited for: 15 -> 24; matrix products, arithmetic and copies ran while one was open for 14% -> 16% of each run, Pallas kernels for 0% -> 0%
where the time goes in v1:
time: 1670 us; the launch traced here: 1660 us
  waiting for transfers between devices  973 us (58%)
  local copies, waits for them, and re-layouts  225 us (13%)
  matrix products  177 us (11%)
  blocking collectives  165 us (10%)
  other arithmetic  58.2 us (3%)
  starting transfers between devices  39.5 us (2%)
  between operations  17.5 us (1%)
    unnamed x23, waiting for transfers between devices  391 us
    reduce_scatter x1, waiting for transfers between devices, reduce_weight_grads(): lax.psum_scatter(gradients[6], 'dp', scatter_dimension=0, tiled=True)  143 us
    reduce_scatter x1, waiting for transfers between devices, reduce_weight_grads(): lax.psum_scatter(gradients[2], 'dp', scatter_dimension=0, tiled=True)  129 us
    reduce_scatter x1, waiting for transfers between devices, reduce_weight_grads(): lax.psum_scatter(gradients[3], 'dp', scatter_dimension=0, tiled=True)  129 us
    reduce_scatter x1, waiting for transfers between devices, reduce_weight_grads(): lax.psum_scatter(gradients[5], 'dp', scatter_dimension=0, tiled=True)  125 us
    unnamed x302, local copies, waits for them, and re-layouts  66.5 us
    all_gather x1, blocking collectives, fetch_weights(): lax.all_gather(cross_query_weight, 'dp', axis=0, tiled=True)  42.9 us
    all_gather x1, blocking collectives, fetch_weights(): lax.all_gather(norm_gains, 'dp', axis=1, tiled=True)  42.4 us
  transfers between devices with their start and end apart: 33, of which 24 were waited for; matrix products, arithmetic and copies ran while one was open for 16% of the time, Pallas kernels for 0%

profile of v1, /device:TPU:0, one launch (start us, length us, event | category | flops | bytes accessed | tf_op | source)
XLA Modules:
  0.0 1656.7 jit_solution(173063561199506076)
XLA Ops:
  11.9 42.4 %all-gather = bf16[16,48,3]{1,2,0:T(4,128)(2,1)S(1)} all-gather(bf16[1,48,3]{1,2,0:T(4,128)(2,1)S(1)} %bitcast.350), channel_id=1, replica_groups=mesh['dp'=16,'mp'=2] {'dp'}, dimensions={0}, use_global_device_ids=true | all-gather | bytes 4896 | tf_op jit(solution)/shard_map/all_gather | solution.py:110
  56.9 40.3 %all_gather.30 = bf16[768,384]{1,0:T(8,128)(2,1)S(1)} all-gather(bf16[48,384]{1,0:T(8,128)(2,1)S(1)} %copy-done.98), channel_id=1, replica_groups=mesh['dp'=16,'mp'=2] {'dp'}, dimensions={0}, use_global_device_ids=true | all-gather | bytes 626688 | tf_op jit(solution)/shard_map/all_gather | solution.py:112
  97.3 42.9 %all_gather.32 = bf16[768,384]{1,0:T(8,128)(2,1)S(1)} all-gather(bf16[48,384]{1,0:T(8,128)(2,1)S(1)} %copy-done.99), channel_id=1, replica_groups=mesh['dp'=16,'mp'=2] {'dp'}, dimensions={0}, use_global_device_ids=true | all-gather | bytes 626688 | tf_op jit(solution)/shard_map/all_gather | solution.py:113
  140.2 39.6 %all_gather.33 = bf16[768,384]{1,0:T(8,128)(2,1)S(1)} all-gather(bf16[48,384]{1,0:T(8,128)(2,1)S(1)} %copy-done.100), channel_id=1, replica_groups=mesh['dp'=16,'mp'=2] {'dp'}, dimensions={0}, use_global_device_ids=true | all-gather | bytes 626688 | tf_op jit(solution)/shard_map/all_gather | solution.py:115
  296.6 6.2 collective-permute-start.5
  306.7 6.1 collective-permute-start.7
  316.8 6.1 collective-permute-start.9
  325.6 6.2 collective-permute-start.11
  335.3 6.1 collective-permute-start.13
  345.1 7.4 collective-permute-done.12
  353.9 10.5 collective-permute-done.14
  375.4 6.4 add_convert_fusion
  416.3 19.6 %all-reduce.19.cloned.1.call-done = (f32[256,768]{1,0:T(8,128)}, f32[256,768]{1,0:T(8,128)}) async-done(((f32[256,768]{1,0:T(8,128)}, f32[256,768]{1,0:T(8,128)}), (f32[256,768]{1,0:T(8,128)}, f32[256,768]{1,0:T(8,128)})) %all-reduce.19.cloned.1.call-update) | async-done | bytes 1572880 | tf_op jit(solution)/shard_map/psum | solution.py:135
  494.5 6.3 copy.329
  570.7 6.2 copy.328
  576.9 10.9 fusion.16
  601.9 6.6 copy.374
  618.7 6.1 copy.334
  629.1 6.2 copy.333
  635.2 10.1 fusion.19
  649.4 6.6 copy.376
  668.4 5.3 copy.341
  678.2 6.2 copy.338
  705.2 6.0 copy.380
  721.5 9.4 reduce-scatter.25.cloned.1.call-done
  735.4 8.1 reduce-scatter.27.cloned.1.call-done
  750.1 229.6 %all-reduce.17.cloned.1.call-done = (f32[3,768,384]{2,0,1:T(4,128)}, f32[2,768,384]{2,0,1:T(2,128)}) async-done(((f32[3,768,384]{2,0,1:T(4,128)}, f32[2,768,384]{2,0,1:T(2,128)}), (f32[3,768,384]{2,0,1:T(4,128)}, f32[2,768,384]{2,0,1:T(2,128)})) %all-reduce.17.cloned.1.call-update) | async-done | bytes 5898256
  983.0 125.3 %reduce-scatter.21.cloned.1.call-done = f32[48,384]{1,0:T(8,128)} async-done(((f32[768,384]{1,0:T(8,128)}), f32[48,384]{1,0:T(8,128)}) %reduce-scatter.21.cloned.1.call-update) | async-done | bytes 73744 | tf_op jit(solution)/shard_map/reduce_scatter | solution.py:128
  1108.3 128.6 %reduce-scatter.19.cloned.1.call-done = f32[48,384]{1,0:T(8,128)} async-done(((f32[768,384]{1,0:T(8,128)}), f32[48,384]{1,0:T(8,128)}) %reduce-scatter.19.cloned.1.call-update) | async-done | bytes 73744 | tf_op jit(solution)/shard_map/reduce_scatter | solution.py:126
  1236.8 128.6 %reduce-scatter.17.cloned.1.call-done = f32[48,384]{1,0:T(8,128)} async-done(((f32[768,384]{1,0:T(8,128)}), f32[48,384]{1,0:T(8,128)}) %reduce-scatter.17.cloned.1.call-update) | async-done | bytes 73744 | tf_op jit(solution)/shard_map/reduce_scatter | solution.py:125
  1365.5 142.6 %reduce-scatter.23.cloned.1.call-done = f32[48,1536]{1,0:T(8,128)} async-done(((f32[768,1536]{1,0:T(8,128)}), f32[48,1536]{1,0:T(8,128)}) %reduce-scatter.23.cloned.1.call-update) | async-done | bytes 294928 | tf_op jit(solution)/shard_map/reduce_scatter | solution.py:129
  1508.0 141.4 %reduce-scatter.31.cloned.1.call-done = f32[48,1536]{1,0:T(8,128)} async-done(((f32[768,1536]{1,0:T(8,128)}), f32[48,1536]{1,0:T(8,128)}) %reduce-scatter.31.cloned.1.call-update) | async-done | bytes 294928
  (594 shorter events, 409.3 us)
Async XLA Ops:
  7.2 172.7 %all-gather.7.cloned.1.call-start = ((), (), s32[]{:S(2)}) async-start(), calls=%async_computation.9 | async-start | bytes 1253376 | tf_op jit(solution)/shard_map/all_gather | solution.py:114
  8.0 181.1 %all-gather.5.cloned.1.call-start = ((), (), s32[]{:S(2)}) async-start(), calls=%async_computation.8 | async-start | bytes 1880064 | tf_op jit(solution)/shard_map/all_gather | solution.py:111
  8.7 239.7 %all-reduce.23.cloned.1.call-start = ((), (), s32[]{:S(2)}) async-start(), calls=%async_computation.22 | async-start | bytes 3145728 | tf_op jit(solution)/shard_map/psum | solution.py:135
  214.4 150.7 %all-reduce.21.cloned.1.call-start = ((), (), s32[]{:S(2)}) async-start(), calls=%async_computation.21 | async-start | bytes 3145728 | tf_op jit(solution)/shard_map/psum | solution.py:135
  281.4 94.0 %all-gather.9.cloned.1.call-start = ((), (), s32[]{:S(2)}) async-start(), calls=%async_computation.10 | async-start | bytes 2506752 | tf_op jit(solution)/shard_map/all_gather | solution.py:117
  281.5 7.7 collective-permute-start.1
  282.9 11.1 collective-permute-start
  283.6 127.5 %all-reduce.29.cloned.1.call-start = ((), (), s32[]{:S(2)}) async-start(), calls=%async_computation.25 | async-start | bytes 1572864 | tf_op jit(solution)/shard_map/psum | solution.py:139
  293.9 9.1 collective-permute-start.2
  296.6 10.1 collective-permute-start.5
  303.0 10.3 collective-permute-start.4
  306.7 10.1 collective-permute-start.7
  313.3 10.6 collective-permute-start.6
  316.8 8.8 collective-permute-start.9
  323.9 8.8 collective-permute-start.8
  325.6 9.7 collective-permute-start.11
  332.8 11.0 collective-permute-start.10
  335.3 17.9 %collective-permute-start.13 = (bf16[48,1536]{1,0:T(8,128)(2,1)S(1)}, bf16[48,1536]{1,0:T(8,128)(2,1)S(1)}, u32[]{:S(2)}, u32[]{:S(2)}) collective-permute-start(bf16[48,1536]{1,0:T(8,128)(2,1)S(1)} %collective-permute-done.11), channel_id=1, source_target_pairs={{0,30},{2,0},{4,2},{6,4},{8,6},{10,8},{12,10},{14,12},{16,14},{18,... | collective-permute-start | bytes 442376 | tf_op jit(solution)/shard_map/ppermute | solution.py:23
  343.8 8.7 collective-permute-start.12
  352.5 11.9 collective-permute-start.14
  395.8 40.0 %all-reduce.19.cloned.1.call-start = ((), (), s32[]{:S(2)}) async-start(), calls=%async_computation.20 | async-start | bytes 3145728 | tf_op jit(solution)/shard_map/psum | solution.py:135
  403.4 101.2 %all-reduce.27.cloned.1.call-start = ((), (), s32[]{:S(2)}) async-start(), calls=%async_computation.24 | async-start | bytes 1572864 | tf_op jit(solution)/shard_map/psum | solution.py:139
  484.1 104.9 %all-reduce.25.cloned.1.call-start = ((), (), s32[]{:S(2)}) async-start(), calls=%async_computation.23 | async-start | bytes 1572864 | tf_op jit(solution)/shard_map/psum | solution.py:139
  566.0 154.2 %reduce-scatter.29.cloned.1.call-start = ((), (), s32[]{:S(2)}) async-start(), calls=%async_computation.17 | async-start | bytes 417792
  597.2 133.7 %reduce-scatter.25.cloned.1.call-start = ((), (), s32[]{:S(2)}) async-start(), calls=%async_computation.15 | async-start | bytes 2654208
  613.5 130.1 %reduce-scatter.27.cloned.1.call-start = ((), (), s32[]{:S(2)}) async-start(), calls=%async_computation.16 | async-start | bytes 2654208
  660.9 318.8 %all-reduce.17.cloned.1.call-start = ((), (), s32[]{:S(2)}) async-start(), calls=%async_computation.19 | async-start | bytes 14155776
  684.5 423.8 %reduce-scatter.21.cloned.1.call-start = ((), (), s32[]{:S(2)}) async-start(), calls=%async_computation.13 | async-start | bytes 1253376 | tf_op jit(solution)/shard_map/reduce_scatter | solution.py:128
  687.6 549.3 %reduce-scatter.19.cloned.1.call-start = ((), (), s32[]{:S(2)}) async-start(), calls=%async_computation.12 | async-start | bytes 1253376 | tf_op jit(solution)/shard_map/reduce_scatter | solution.py:126
  691.5 673.9 %reduce-scatter.17.cloned.1.call-start = ((), (), s32[]{:S(2)}) async-start(), calls=%async_computation.11 | async-start | bytes 1253376 | tf_op jit(solution)/shard_map/reduce_scatter | solution.py:125
  694.5 813.5 %reduce-scatter.23.cloned.1.call-start = ((), (), s32[]{:S(2)}) async-start(), calls=%async_computation.14 | async-start | bytes 5013504 | tf_op jit(solution)/shard_map/reduce_scatter | solution.py:129
  700.0 949.4 %reduce-scatter.31.cloned.1.call-start = ((), (), s32[]{:S(2)}) async-start(), calls=%async_computation.18 | async-start | bytes 5013504
  (142 other events, 2026.8 us)
Sparse Core Ops, SparseCore 0:
  10.7 59.4 all-gather.6
  72.9 61.6 all-gather.4
  214.5 17.3 all-reduce.22
  281.5 17.5 all-reduce.20
  301.8 68.1 all-gather.8
  395.9 15.1 all-reduce.28
  414.2 21.6 all-reduce.18
  484.2 20.4 all-reduce.26
  566.1 20.4 all-reduce.24
  597.3 122.7 reduce-scatter.28
  722.5 8.3 reduce-scatter.24
  733.0 10.4 reduce-scatter.26
  751.1 228.5 all-reduce.16
  985.6 122.6 reduce-scatter.20
  1114.2 122.6 reduce-scatter.18
  1242.7 122.6 reduce-scatter.16
  1371.9 136.1 reduce-scatter.22
  1513.6 135.7 reduce-scatter.30
